TPU v7x, 32 devices: a whole 2x2x4 slice. The times are simulated.
32 devices in a mesh: section: 2 (over x), req: 8 (over z, y), head: 2 (over core).
Axes of the slice: x: 2, y: 2, z: 4, core: 2. Of those that a mesh axis runs over, the one named last changes fastest.
Arguments:
- latent_tokens: bfloat16 [8, 2, 256, 1536], P('req', None, 'head'), may hold values from -6 to 6
- w_qkv: bfloat16 [2, 1536, 4608], P('section', 'req', 'head'), may hold values from -0.15625 to 0.15625
- w_out: bfloat16 [2, 1536, 1536], P('section', 'head', 'req'), may hold values from -0.75 to 0.75
- time_mod: float32 [2, 28, 3, 1536], P('section'), may hold values from -3 to 3
- text_mod: float32 [2, 8, 2, 3, 1536], P('section', 'req'), may hold values from -3 to 3
- stale_kv: bfloat16 [2, 8, 2, 1178, 3072], P('section', 'req', None, None, 'head'), may hold values from -150 to 150
- guided: int32 [8], P('req'), may hold values 0 or 1
- patch_index: int32 [8], P('req'), may hold values from 0 to 3
- timestep: int32 [8], P('req'), may hold values from 0 to 27
Outputs:
- hidden_out: bfloat16 [2, 8, 2, 256, 1536], P('section', 'req', None, 'head')
- fresh_kv: bfloat16 [2, 8, 2, 256, 3072], P('section', 'req', None, None, 'head')
All inputs are finite; a program needn't handle non-finite values. No bound on the sum of `guided` on one device may be relied on, other than what follows from the above.
Results may differ from a plain program's by a relative error of at most 0.04.
Values may be sent and summed in bfloat16 or wider, within the bound.
A program may use at most 192 MiB of HBM per device.

v0:
```python
import jax
import jax.numpy as jnp
from jax import lax
from jax.sharding import PartitionSpec as P

HD = 64
PATCH = 256
PATCHES = 4
STALE = 1178


def shifted(block, axis, distance):
    devices = range(lax.axis_size(axis))
    route = [(i - distance, i) for i in devices if i - distance in devices]
    return lax.ppermute(block, axis, route)


def attend(queries, own_keys, own_values, stale_pair, patch_here):
    heads_here = queries.shape[1]
    stale_split = stale_pair.reshape(STALE, heads_here, 2, HD)
    stale_keys = stale_split[:, :, 0]
    stale_values = stale_split[:, :, 1]
    all_keys = jnp.concatenate([own_keys, stale_keys], 0)
    all_values = jnp.concatenate([own_values, stale_values], 0)
    scores = jnp.einsum(
        "qhd,khd->hqk", queries, all_keys, preferred_element_type=jnp.float32
    ) * HD ** (-0.5)
    position = jnp.arange(PATCH + STALE, dtype=jnp.int32)
    stale_pos = position - PATCH
    hidden_key = (
        (stale_pos >= 0) & (stale_pos < PATCHES * PATCH) & (stale_pos // PATCH == patch_here)
    )
    scores = jnp.where(hidden_key[None, None, :], -jnp.inf, scores)
    row_max = jnp.max(scores, axis=-1, keepdims=True)
    exponent = jnp.exp(scores - row_max)
    weights = (exponent / jnp.sum(exponent, axis=-1, keepdims=True)).astype(jnp.bfloat16)
    mixed_heads = jnp.einsum(
        "hqk,khd->qhd", weights, all_values, preferred_element_type=jnp.float32
    )
    return mixed_heads.astype(jnp.bfloat16).reshape(PATCH, heads_here * HD)


def shards(
    latent_tokens, w_qkv, w_out, time_mod, text_mod, stale_kv, guided, patch_index, timestep
):
    section_index = lax.axis_index("section")
    requests = latent_tokens.shape[0]
    item_count = 2 * requests
    local_rows = latent_tokens.shape[2]
    model_width = latent_tokens.shape[3]
    pair_cols = stale_kv.shape[-1]
    feature_cols = pair_cols // 2
    heads_here = feature_cols // HD
    table_rows = time_mod.shape[1]
    tokens = latent_tokens.reshape(item_count, local_rows, model_width)
    picker = (timestep[:, None] == jnp.arange(table_rows, dtype=jnp.int32)[None, :]).astype(
        jnp.float32
    )
    per_time = jnp.einsum("rt,tcd->rcd", picker, time_mod[0], precision=lax.Precision.HIGHEST)
    modulation = (per_time[:, None] + text_mod[0]).reshape(item_count, 3, model_width)
    stale_all = stale_kv[0].reshape(item_count, STALE, pair_cols)
    patch_all = jnp.repeat(patch_index, 2)
    guided_all = jnp.repeat(guided, 2)
    parity = jnp.arange(item_count, dtype=jnp.int32) % 2
    keep_all = jnp.where((parity == 1) & (guided_all == 0), 0.0, 1.0).astype(jnp.float32)
    qkv_full, out_full = (
        lax.all_gather(w_qkv[0], "req", axis=0, tiled=True),
        lax.all_gather(w_out[0], "req", axis=1, tiled=True),
    )

    def project_in(normed):
        return jnp.dot(normed, qkv_full, preferred_element_type=jnp.float32)

    def project_out(mixed_heads):
        return jnp.dot(mixed_heads, out_full, preferred_element_type=jnp.float32)

    def tick_step(tick_index, state_tuple):
        sent, hidden_buf, fresh_buf = state_tuple
        received = shifted(sent, "section", 1)
        item_index = tick_index - section_index
        in_range = (item_index >= 0) & (item_index < item_count)
        slot_index = jnp.clip(item_index, 0, item_count - 1)
        own_tokens = lax.dynamic_index_in_dim(tokens, slot_index, 0, keepdims=False)
        layer_in = jnp.where(section_index == 0, own_tokens, received)
        gathered = lax.all_gather(layer_in, "head", axis=0, tiled=True)
        mod_here = lax.dynamic_index_in_dim(modulation, slot_index, 0, keepdims=False)
        values_f = gathered.astype(jnp.float32)
        row_mean = jnp.mean(values_f, axis=-1, keepdims=True)
        centered = values_f - row_mean
        row_var = jnp.mean(centered * centered, axis=-1, keepdims=True)
        normed = (centered * lax.rsqrt(row_var + 1e-06) * (1.0 + mod_here[1]) + mod_here[0]).astype(
            jnp.bfloat16
        )
        projected = project_in(normed).reshape(PATCH, heads_here, 3, HD)
        queries = projected[:, :, 0].astype(jnp.bfloat16)
        own_keys = projected[:, :, 1].astype(jnp.bfloat16)
        own_values = projected[:, :, 2].astype(jnp.bfloat16)
        stale_pair = lax.dynamic_index_in_dim(stale_all, slot_index, 0, keepdims=False)
        patch_here = lax.dynamic_index_in_dim(patch_all, slot_index, 0, keepdims=False)
        keep_here = lax.dynamic_index_in_dim(keep_all, slot_index, 0, keepdims=False)
        mixed_heads = attend(queries, own_keys, own_values, stale_pair, patch_here)
        out_terms = project_out(mixed_heads)
        attn_part = lax.psum_scatter(
            out_terms.astype(jnp.bfloat16), "head", scatter_dimension=0, tiled=True
        ).astype(jnp.float32)
        updated = (layer_in.astype(jnp.float32) + mod_here[2] * attn_part).astype(jnp.bfloat16)
        kept_rows = (updated.astype(jnp.float32) * keep_here).astype(jnp.bfloat16)
        previous = lax.dynamic_index_in_dim(hidden_buf, slot_index, 0, keepdims=False)
        stored_rows = jnp.where(in_range, kept_rows, previous)
        hidden_buf = lax.dynamic_update_index_in_dim(hidden_buf, stored_rows, slot_index, 0)
        fresh_pair = jnp.stack([own_keys, own_values], axis=2).reshape(PATCH, pair_cols)
        kept_fresh = (fresh_pair.astype(jnp.float32) * keep_here).astype(jnp.bfloat16)
        previous_fresh = lax.dynamic_index_in_dim(fresh_buf, slot_index, 0, keepdims=False)
        stored_fresh = jnp.where(in_range, kept_fresh, previous_fresh)
        fresh_buf = lax.dynamic_update_index_in_dim(fresh_buf, stored_fresh, slot_index, 0)
        return (updated, hidden_buf, fresh_buf)

    start_state = (
        jnp.zeros((local_rows, model_width), jnp.bfloat16),
        jnp.zeros((item_count, local_rows, model_width), jnp.bfloat16),
        jnp.zeros((item_count, PATCH, pair_cols), jnp.bfloat16),
    )
    finished = lax.fori_loop(0, item_count + 1, tick_step, start_state)
    hidden_out = finished[1].reshape(1, requests, 2, local_rows, model_width)
    fresh_kv = finished[2].reshape(1, requests, 2, PATCH, pair_cols)
    return (hidden_out, fresh_kv)


def solution(mesh):
    in_specs = (
        P("req", None, "head", None),
        P("section", "req", "head"),
        P("section", "head", "req"),
        P("section", None, None, None),
        P("section", "req", None, None, None),
        P("section", "req", None, None, "head"),
        P("req"),
        P("req"),
        P("req"),
    )
    out_specs = (P("section", "req", None, "head", None), P("section", "req", None, None, "head"))
    return jax.shard_map(shards, mesh=mesh, in_specs=in_specs, out_specs=out_specs, check_vma=False)
```

profile of v0, /device:TPU:0, one launch (start us, length us, event | category | flops | bytes accessed | tf_op | source)
XLA Modules:
  0.0 409.9 jit_solution(2994836607392291890)
XLA Ops:
  8.7 20.0 %copy.38 = bf16[1,1,2,1178,1536]{3,4,2,1,0:T(8,128)(2,1)} copy(bf16[1,1,2,1178,1536]{4,2,3,1,0:T(2,128)(2,1)} %param.16) | data formatting | bytes 14475264 | tf_op args[5]
  31.7 33.3 %all-gather.7.cloned.1.call-done = bf16[1,768,1536]{1,2,0:T(8,128)(2,1)} async-done(((bf16[1,768,192]{1,2,0:T(8,128)(2,1)}), bf16[1,768,1536]{1,2,0:T(8,128)(2,1)}) %all-gather.7.cloned.1.call-update) | async-done | bytes 2359312 | tf_op jit(solution)/shard_map/all_gather | solution.py:68
  65.0 4.3 %copy.39 = bf16[768,1536]{1,0:T(8,128)(2,1)} copy(bf16[768,1536]{0,1:T(8,128)(2,1)} %bitcast.102) | data formatting | bytes 4718592
  69.3 105.3 %all-gather.5.cloned.1.call-done = bf16[1,1536,2304]{2,1,0:T(8,128)(2,1)} async-done(((bf16[1,192,2304]{2,1,0:T(8,128)(2,1)}), bf16[1,1536,2304]{2,1,0:T(8,128)(2,1)}) %all-gather.5.cloned.1.call-update) | async-done | bytes 7077904 | tf_op jit(solution)/shard_map/all_gather | solution.py:67
  177.3 226.1 %while.20 = (s32[]{:T(128)}, bf16[128,1536]{1,0:T(8,128)(2,1)}, bf16[2,128,1536]{2,1,0:T(8,128)(2,1)}, bf16[2,256,1536]{2,1,0:T(8,128)(2,1)}, pred[]{:T(512)}, /...) while((s32[]{:T(128)}, bf16[128,1536]{1,0:T(8,128)(2,1)}, ...), condition=%wide.region_6.7_spmd.clone, body=%wide.region_0.6_spmd.clone.sunk | while | flops 3597972224 | bytes 154106176 | solution.py:123
  177.3 3.4 collective-permute-start
  192.6 6.1 %fusion.87 = bf16[256,2304]{0,1:T(8,128)(2,1)S(1)} fusion(bf16[1536,2304]{1,0:T(8,128)(2,1)} %get-tuple-element.539, bf16[256,1536]{1,0:T(8,128)(2,1)S(1)} %all_gather.20, f32[1536]{0:T(1024)S(1)} %get-tuple-element.484, f32[1536]{0:T(1024)S(1)} %get-tuple-element.485, f32[256]{0:T(256)S(1)} %add_rsqrt_fusion.2, f32[256]{0:T(256)S(1)} %broadcast_multiply_fusion.2), kind=kOutput, calls=%fused_computation.29.clone.1 | convolution fusion | flops 1814298624 | bytes 9058304 | tf_op jit(solution)/shard_map/while/body/eval_jaxpr/dot_general | solution.py:72
  198.8 8.5 %fusion.89 = f32[12,256,1434]{1,2,0:T(8,128)} fusion(bf16[1178,12,64]{0,2,1:T(8,128)(2,1)S(1)} %get-tuple-element.483, bf16[256,12,64]{0,2,1:T(8,128)(2,1)S(1)} %bitcast.95, bf16[256,12,1,64]{0,3,2,1:T(8,128)(2,1)S(1)} %get-tuple-element.487), kind=kOutput, calls=%fused_computation.13.clone.1 | convolution fusion | flops 568276992 | bytes 20216832 | tf_op jit(solution)/shard_map/while/body/eval_jaxpr/qhd,khd->hqk/dot_general | solution.py:25
  207.4 21.2 %fusion.91 = (f32[12,256]{1,0:T(8,128)}, f32[12,256,1434]{1,2,0:T(8,128)}) fusion(f32[12,256,1434]{1,2,0:T(8,128)} %fusion.89, pred[1434]{0:T(1024)(128)(4,1)S(1)} %fusion.90), kind=kOutput, calls=%fused_computation.86.clone.1 | output fusion | flops 26432920 | bytes 35255704 | tf_op jit(solution)/shard_map/while/body/eval_jaxpr/sub | solution.py:35
  228.6 7.9 %fusion.92 = bf16[12,64,256]{2,1,0:T(8,128)(2,1)S(1)} fusion(f32[12,256,1434]{1,2,0:T(8,128)} %get-tuple-element.488, f32[12,256]{1,0:T(8,128)} %get-tuple-element.489, bf16[1178,12,64]{0,2,1:T(8,128)(2,1)S(1)} %copy-done.1, bf16[256,12,64]{0,2,1:T(8,128)(2,1)S(1)} %bitcast.99), kind=kOutput, calls=%fused_computation.28.clone.1 | convolution fusion | flops 577284096 | bytes 20229120 | tf_op jit(solution)/shard_map/while/body/eval_jaxpr/hqk,khd->qhd/dot_general | solution.py:37
  243.5 2.8 reduce-scatter.2.cloned.1.call-done
  246.3 2.6 fusion.93
  250.8 3.6 collective-permute-start
  267.2 6.1 %fusion.87 = bf16[256,2304]{0,1:T(8,128)(2,1)S(1)} fusion(bf16[1536,2304]{1,0:T(8,128)(2,1)} %get-tuple-element.539, bf16[256,1536]{1,0:T(8,128)(2,1)S(1)} %all_gather.20, f32[1536]{0:T(1024)S(1)} %get-tuple-element.484, f32[1536]{0:T(1024)S(1)} %get-tuple-element.485, f32[256]{0:T(256)S(1)} %add_rsqrt_fusion.2, f32[256]{0:T(256)S(1)} %broadcast_multiply_fusion.2), kind=kOutput, calls=%fused_computation.29.clone.1 | convolution fusion | flops 1814298624 | bytes 9058304 | tf_op jit(solution)/shard_map/while/body/eval_jaxpr/dot_general | solution.py:72
  273.5 8.5 %fusion.89 = f32[12,256,1434]{1,2,0:T(8,128)} fusion(bf16[1178,12,64]{0,2,1:T(8,128)(2,1)S(1)} %get-tuple-element.483, bf16[256,12,64]{0,2,1:T(8,128)(2,1)S(1)} %bitcast.95, bf16[256,12,1,64]{0,3,2,1:T(8,128)(2,1)S(1)} %get-tuple-element.487), kind=kOutput, calls=%fused_computation.13.clone.1 | convolution fusion | flops 568276992 | bytes 20216832 | tf_op jit(solution)/shard_map/while/body/eval_jaxpr/qhd,khd->hqk/dot_general | solution.py:25
  282.0 21.2 %fusion.91 = (f32[12,256]{1,0:T(8,128)}, f32[12,256,1434]{1,2,0:T(8,128)}) fusion(f32[12,256,1434]{1,2,0:T(8,128)} %fusion.89, pred[1434]{0:T(1024)(128)(4,1)S(1)} %fusion.90), kind=kOutput, calls=%fused_computation.86.clone.1 | output fusion | flops 26432920 | bytes 35255704 | tf_op jit(solution)/shard_map/while/body/eval_jaxpr/sub | solution.py:35
  303.2 7.9 %fusion.92 = bf16[12,64,256]{2,1,0:T(8,128)(2,1)S(1)} fusion(f32[12,256,1434]{1,2,0:T(8,128)} %get-tuple-element.488, f32[12,256]{1,0:T(8,128)} %get-tuple-element.489, bf16[1178,12,64]{0,2,1:T(8,128)(2,1)S(1)} %copy-done.1, bf16[256,12,64]{0,2,1:T(8,128)(2,1)S(1)} %bitcast.99), kind=kOutput, calls=%fused_computation.28.clone.1 | convolution fusion | flops 577284096 | bytes 20229120 | tf_op jit(solution)/shard_map/while/body/eval_jaxpr/hqk,khd->qhd/dot_general | solution.py:37
  318.1 5.0 %reduce-scatter.2.cloned.1.call-done = bf16[128,1536]{1,0:T(8,128)(2,1)} async-done(((bf16[256,1536]{1,0:T(8,128)(2,1)}), bf16[128,1536]{1,0:T(8,128)(2,1)}) %reduce-scatter.2.cloned.1.call-update) | async-done | bytes 393232 | tf_op jit(solution)/shard_map/while/body/eval_jaxpr/reduce_scatter | solution.py:103
  327.6 3.6 collective-permute-start
  344.0 6.1 %fusion.87 = bf16[256,2304]{0,1:T(8,128)(2,1)S(1)} fusion(bf16[1536,2304]{1,0:T(8,128)(2,1)} %get-tuple-element.539, bf16[256,1536]{1,0:T(8,128)(2,1)S(1)} %all_gather.20, f32[1536]{0:T(1024)S(1)} %get-tuple-element.484, f32[1536]{0:T(1024)S(1)} %get-tuple-element.485, f32[256]{0:T(256)S(1)} %add_rsqrt_fusion.2, f32[256]{0:T(256)S(1)} %broadcast_multiply_fusion.2), kind=kOutput, calls=%fused_computation.29.clone.1 | convolution fusion | flops 1814298624 | bytes 9058304 | tf_op jit(solution)/shard_map/while/body/eval_jaxpr/dot_general | solution.py:72
  350.3 8.5 %fusion.89 = f32[12,256,1434]{1,2,0:T(8,128)} fusion(bf16[1178,12,64]{0,2,1:T(8,128)(2,1)S(1)} %get-tuple-element.483, bf16[256,12,64]{0,2,1:T(8,128)(2,1)S(1)} %bitcast.95, bf16[256,12,1,64]{0,3,2,1:T(8,128)(2,1)S(1)} %get-tuple-element.487), kind=kOutput, calls=%fused_computation.13.clone.1 | convolution fusion | flops 568276992 | bytes 20216832 | tf_op jit(solution)/shard_map/while/body/eval_jaxpr/qhd,khd->hqk/dot_general | solution.py:25
  358.8 21.2 %fusion.91 = (f32[12,256]{1,0:T(8,128)}, f32[12,256,1434]{1,2,0:T(8,128)}) fusion(f32[12,256,1434]{1,2,0:T(8,128)} %fusion.89, pred[1434]{0:T(1024)(128)(4,1)S(1)} %fusion.90), kind=kOutput, calls=%fused_computation.86.clone.1 | output fusion | flops 26432920 | bytes 35255704 | tf_op jit(solution)/shard_map/while/body/eval_jaxpr/sub | solution.py:35
  380.0 7.9 %fusion.92 = bf16[12,64,256]{2,1,0:T(8,128)(2,1)S(1)} fusion(f32[12,256,1434]{1,2,0:T(8,128)} %get-tuple-element.488, f32[12,256]{1,0:T(8,128)} %get-tuple-element.489, bf16[1178,12,64]{0,2,1:T(8,128)(2,1)S(1)} %copy-done.1, bf16[256,12,64]{0,2,1:T(8,128)(2,1)S(1)} %bitcast.99), kind=kOutput, calls=%fused_computation.28.clone.1 | convolution fusion | flops 577284096 | bytes 20229120 | tf_op jit(solution)/shard_map/while/body/eval_jaxpr/hqk,khd->qhd/dot_general | solution.py:37
  394.9 5.0 %reduce-scatter.2.cloned.1.call-done = bf16[128,1536]{1,0:T(8,128)(2,1)} async-done(((bf16[256,1536]{1,0:T(8,128)(2,1)}), bf16[128,1536]{1,0:T(8,128)(2,1)}) %reduce-scatter.2.cloned.1.call-update) | async-done | bytes 393232 | tf_op jit(solution)/shard_map/while/body/eval_jaxpr/reduce_scatter | solution.py:103
  (126 shorter events, 73.7 us)
Async XLA Ops:
  7.2 57.8 %all-gather.7.cloned.1.call-start = ((), (), s32[]{:S(2)}) async-start(), calls=%async_computation.2 | async-start | bytes 2654208 | tf_op jit(solution)/shard_map/all_gather | solution.py:68
  7.9 166.6 %all-gather.5.cloned.1.call-start = ((), (), s32[]{:S(2)}) async-start(), calls=%async_computation.1 | async-start | bytes 7962624 | tf_op jit(solution)/shard_map/all_gather | solution.py:67
  8.7 20.7 %copy-start.4 = (f32[1,28,3,1536]{3,0,2,1:T(1,128)S(1)}, f32[1,28,3,1536]{3,0,2,1:T(1,128)}, u32[]{:S(2)}) copy-start(f32[1,28,3,1536]{3,0,2,1:T(1,128)} %param.14) | copy-start | bytes 1548292
  8.7 22.3 %copy-start.5 = (f32[1,1,2,3,1536]{4,2,3,1,0:T(2,128)S(1)}, f32[1,1,2,3,1536]{4,2,3,1,0:T(2,128)}, u32[]{:S(2)}) copy-start(f32[1,1,2,3,1536]{4,2,3,1,0:T(2,128)} %param.15) | copy-start | bytes 110596
  177.3 69.0 %reduce-scatter.2.cloned.1.call-start = ((), (), s32[]{:S(2)}) async-start(), calls=%async_computation.3 | async-start | bytes 1179648 | tf_op jit(solution)/shard_map/while/body/eval_jaxpr/reduce_scatter | solution.py:103
  177.3 11.3 %collective-permute-start = (bf16[128,1536]{1,0:T(8,128)(2,1)S(1)}, bf16[128,1536]{1,0:T(8,128)(2,1)S(1)}, u32[]{:S(2)}, u32[]{:S(2)}) collective-permute-start(bf16[128,1536]{1,0:T(8,128)(2,1)S(1)} %broadcast_select_fusion.4), channel_id=1, source_target_pairs={{0,16},{1,17},{2,18},{3,19},{4,20},{5,21},{6,22},{7,23},{8,24},{9,... | collective-permute-start | bytes 1179656 | tf_op jit(solution)/shard_map/while/body/eval_jaxpr/ppermute | solution.py:15
  207.4 21.2 %copy-start.1 = (bf16[1178,12,64]{0,2,1:T(8,128)(2,1)S(1)}, bf16[1178,12,64]{0,2,1:T(8,128)(2,1)}, u32[]{:S(2)}) copy-start(bf16[1178,12,64]{0,2,1:T(8,128)(2,1)} %get-tuple-element.490) | copy-start | bytes 5428228 | tf_op jit(solution)/shard_map/while
  228.6 7.9 %copy-start = (bf16[768,1536]{1,0:T(8,128)(2,1)S(1)}, bf16[768,1536]{1,0:T(8,128)(2,1)}, u32[]{:S(2)}) copy-start(bf16[768,1536]{1,0:T(8,128)(2,1)} %get-tuple-element.542) | copy-start | bytes 7077892 | tf_op jit(solution)/shard_map/while
  242.2 4.0 copy-start.2
  248.9 0.9 copy-start.3
  249.7 73.4 %reduce-scatter.2.cloned.1.call-start = ((), (), s32[]{:S(2)}) async-start(), calls=%async_computation.3 | async-start | bytes 1179648 | tf_op jit(solution)/shard_map/while/body/eval_jaxpr/reduce_scatter | solution.py:103
  250.8 12.5 %collective-permute-start = (bf16[128,1536]{1,0:T(8,128)(2,1)S(1)}, bf16[128,1536]{1,0:T(8,128)(2,1)S(1)}, u32[]{:S(2)}, u32[]{:S(2)}) collective-permute-start(bf16[128,1536]{1,0:T(8,128)(2,1)S(1)} %broadcast_select_fusion.4), channel_id=1, source_target_pairs={{0,16},{1,17},{2,18},{3,19},{4,20},{5,21},{6,22},{7,23},{8,24},{9,... | collective-permute-start | bytes 1179656 | tf_op jit(solution)/shard_map/while/body/eval_jaxpr/ppermute | solution.py:15
  282.0 21.2 %copy-start.1 = (bf16[1178,12,64]{0,2,1:T(8,128)(2,1)S(1)}, bf16[1178,12,64]{0,2,1:T(8,128)(2,1)}, u32[]{:S(2)}) copy-start(bf16[1178,12,64]{0,2,1:T(8,128)(2,1)} %get-tuple-element.490) | copy-start | bytes 5428228 | tf_op jit(solution)/shard_map/while
  303.2 7.9 %copy-start = (bf16[768,1536]{1,0:T(8,128)(2,1)S(1)}, bf16[768,1536]{1,0:T(8,128)(2,1)}, u32[]{:S(2)}) copy-start(bf16[768,1536]{1,0:T(8,128)(2,1)} %get-tuple-element.542) | copy-start | bytes 7077892 | tf_op jit(solution)/shard_map/while
  316.9 6.3 %copy-start.2 = (bf16[2,128,1536]{2,1,0:T(8,128)(2,1)S(1)}, bf16[2,128,1536]{2,1,0:T(8,128)(2,1)}, u32[]{:S(2)}) copy-start(bf16[2,128,1536]{2,1,0:T(8,128)(2,1)} %get-tuple-element.515) | copy-start | bytes 2359300 | tf_op jit(solution)/shard_map/while
  325.7 0.9 copy-start.3
  326.6 73.3 %reduce-scatter.2.cloned.1.call-start = ((), (), s32[]{:S(2)}) async-start(), calls=%async_computation.3 | async-start | bytes 1179648 | tf_op jit(solution)/shard_map/while/body/eval_jaxpr/reduce_scatter | solution.py:103
  327.6 12.5 %collective-permute-start = (bf16[128,1536]{1,0:T(8,128)(2,1)S(1)}, bf16[128,1536]{1,0:T(8,128)(2,1)S(1)}, u32[]{:S(2)}, u32[]{:S(2)}) collective-permute-start(bf16[128,1536]{1,0:T(8,128)(2,1)S(1)} %broadcast_select_fusion.4), channel_id=1, source_target_pairs={{0,16},{1,17},{2,18},{3,19},{4,20},{5,21},{6,22},{7,23},{8,24},{9,... | collective-permute-start | bytes 1179656 | tf_op jit(solution)/shard_map/while/body/eval_jaxpr/ppermute | solution.py:15
  358.8 21.2 %copy-start.1 = (bf16[1178,12,64]{0,2,1:T(8,128)(2,1)S(1)}, bf16[1178,12,64]{0,2,1:T(8,128)(2,1)}, u32[]{:S(2)}) copy-start(bf16[1178,12,64]{0,2,1:T(8,128)(2,1)} %get-tuple-element.490) | copy-start | bytes 5428228 | tf_op jit(solution)/shard_map/while
  380.0 7.9 %copy-start = (bf16[768,1536]{1,0:T(8,128)(2,1)S(1)}, bf16[768,1536]{1,0:T(8,128)(2,1)}, u32[]{:S(2)}) copy-start(bf16[768,1536]{1,0:T(8,128)(2,1)} %get-tuple-element.542) | copy-start | bytes 7077892 | tf_op jit(solution)/shard_map/while
  393.7 6.2 %copy-start.2 = (bf16[2,128,1536]{2,1,0:T(8,128)(2,1)S(1)}, bf16[2,128,1536]{2,1,0:T(8,128)(2,1)}, u32[]{:S(2)}) copy-start(bf16[2,128,1536]{2,1,0:T(8,128)(2,1)} %get-tuple-element.515) | copy-start | bytes 2359300 | tf_op jit(solution)/shard_map/while
  402.5 0.9 copy-start.3
Sparse Core Ops, SparseCore 0:
  10.2 54.7 all-gather.6
  67.2 107.3 all-gather.4
  238.3 7.9 reduce-scatter.1
  312.9 10.1 reduce-scatter.1
  389.7 10.1 reduce-scatter.1
where the time goes:
time: 412 us; the launch traced here: 410 us
  waiting for transfers between devices  158 us (38%)
  other arithmetic  86.1 us (21%)
  matrix products  72.6 us (18%)
  local copies, waits for them, and re-layouts  59.1 us (14%)
  between operations  15.7 us (4%)
  starting transfers between devices  10.7 us (3%)
  blocking collectives  7.11 us (2%)
    all_gather x1, waiting for transfers between devices, shards(): lax.all_gather(w_qkv[0], 'req', axis=0, tiled=True)  105 us
    sub x3, other arithmetic, attend(): exponent = jnp.exp(scores - row_max)  63.7 us
    all_gather x1, waiting for transfers between devices, shards(): lax.all_gather(w_out[0], 'req', axis=1, tiled=True)  33.3 us
    dot_general x3, matrix products, attend(): jnp.einsum('qhd,khd->hqk', queries, all_keys, preferred_element_type=jnp....  25.5 us
    unnamed x6, local copies, waits for them, and re-layouts  24.3 us
    dot_general x3, matrix products, attend(): jnp.einsum('hqk,khd->qhd', weights, all_values, preferred_element_type=jn...  23.6 us
    dot_general x3, matrix products, project_in(): return jnp.dot(normed, qkv_full, preferred_element_type=jnp.float32)  18.2 us
    reduce_scatter x3, waiting for transfers between devices, tick_step(): lax.psum_scatter(out_terms.astype(jnp.bfloat16), 'head', scatter_dimensio...  12.8 us
  transfers between devices with their start and end apart: 8, of which 8 were waited for; matrix products, arithmetic and copies ran while one was open for 15% of the time, Pallas kernels for 0%

commit v1 on v0

v1 whole, which is shorter than its diff:
```python
import functools

import jax
import jax.numpy as jnp
from jax import lax
from jax.experimental import pallas as pl
from jax.experimental.pallas import tpu as pltpu
from jax.sharding import PartitionSpec as P

HD = 64
PATCH = 256
PATCHES = 4
STALE = 1178
TEXT = STALE - PATCHES * PATCH
MESH = pl.DeviceIdType.MESH


def ring_index(place, n):
    return jnp.where(place < n // 2, 2 * place, 2 * (n - 1 - place) + 1)


def gather_kernel(n, qkv_ref, out_ref, qkv_all, out_all, send_sem, recv_sem, own_sem):
    me = lax.axis_index("req")
    place = jnp.where(me % 2 == 0, me // 2, n - 1 - me // 2)
    right = ring_index((place + 1) % n, n)
    left = ring_index((place + n - 1) % n, n)
    barrier = pltpu.get_barrier_semaphore()
    for neighbour in (left, right):
        pl.semaphore_signal(barrier, inc=1, device_id={"req": neighbour}, device_id_type=MESH)
    pl.semaphore_wait(barrier, 2)

    rows = qkv_ref.shape[0]
    out_rows = out_ref.shape[0]
    q_half, o_half = rows // 2, out_rows // 2
    q_cut = (q_half // 2 + 7) // 8 * 8
    pieces = []
    for way in range(2):
        pieces.append(
            (
                (qkv_ref, qkv_all, way * q_half, q_cut),
                (qkv_ref, qkv_all, way * q_half + q_cut, q_half - q_cut),
                (out_ref, out_all, way * o_half, o_half),
            )
        )
    own = (
        pltpu.make_async_copy(qkv_ref, qkv_all.at[me], own_sem.at[0]),
        pltpu.make_async_copy(out_ref, out_all.at[me], own_sem.at[1]),
    )

    def hop(step, way, number):
        source, target, first, count = pieces[way][number]
        owner = ring_index((place + (n - step if way == 0 else step)) % n, n)
        span = pl.ds(first, count)
        block = source.at[span] if step == 0 else target.at[owner, span]
        return pltpu.make_async_remote_copy(
            src_ref=block,
            dst_ref=target.at[owner, span],
            send_sem=send_sem.at[way, number],
            recv_sem=recv_sem.at[step, way, number],
            device_id={"req": right if way == 0 else left},
            device_id_type=MESH,
        )

    for step in range(n - 1):
        for number in range(3):
            for way in range(2):
                if step > 0:
                    before = hop(step - 1, way, number)
                    before.wait_recv()
                    before.wait_send()
                hop(step, way, number).start()
        if step == 0:
            for copy in own:
                copy.start()
    for number in range(3):
        for way in range(2):
            last = hop(n - 2, way, number)
            last.wait_recv()
            last.wait_send()
    for copy in own:
        copy.wait()


def gather_weights(qkv_shard, out_shard):
    n = lax.axis_size("req")
    return pl.pallas_call(
        functools.partial(gather_kernel, n),
        out_shape=(
            jax.ShapeDtypeStruct((n, *qkv_shard.shape), qkv_shard.dtype),
            jax.ShapeDtypeStruct((n, *out_shard.shape), out_shard.dtype),
        ),
        in_specs=[pl.BlockSpec(memory_space=pl.ANY)] * 2,
        out_specs=[pl.BlockSpec(memory_space=pl.ANY)] * 2,
        scratch_shapes=[
            pltpu.SemaphoreType.DMA((2, 3)),
            pltpu.SemaphoreType.DMA((n - 1, 2, 3)),
            pltpu.SemaphoreType.DMA((2,)),
        ],
        compiler_params=pltpu.CompilerParams(collective_id=0, has_side_effects=True),
    )(qkv_shard, out_shard)


def nt_dot(a, b):
    return lax.dot_general(a, b, (((1,), (1,)), ((), ())), preferred_element_type=jnp.float32)


def layer_kernel(
    block_heads, facts, hidden, mod, w_qkv, stale, w_out, *rest
):
    fresh_out, out_terms, normed, total = rest[-4:]
    step = pl.program_id(0)

    @pl.when(step == 0)
    def _():
        values_f = hidden[...].astype(jnp.float32)
        row_mean = jnp.mean(values_f, axis=-1, keepdims=True)
        centered = values_f - row_mean
        row_var = jnp.mean(centered * centered, axis=-1, keepdims=True)
        scaled = centered * lax.rsqrt(row_var + 1e-06)
        normed[...] = (scaled * (1.0 + mod[1:2, :]) + mod[0:1, :]).astype(jnp.bfloat16)

    projected = jnp.dot(normed[...], w_qkv[...], preferred_element_type=jnp.float32).astype(
        jnp.bfloat16
    )
    patch_here = facts[1]
    keep = facts[2].astype(jnp.float32)
    blank = jnp.zeros((PATCH, HD), jnp.bfloat16)
    mixed = []
    for head in range(block_heads):
        query = projected[:, head * 3 * HD : head * 3 * HD + HD]
        pair = projected[:, head * 3 * HD + HD : (head + 1) * 3 * HD]
        lanes = slice(head * 2 * HD, (head + 1) * 2 * HD)
        fresh_out[:, lanes] = (pair.astype(jnp.float32) * keep).astype(jnp.bfloat16)
        query = jnp.concatenate([query * jnp.bfloat16(HD**-0.5), blank], axis=1)
        pairs = [pair]
        for number in range(PATCHES - 1):
            place = number + (number >= patch_here).astype(jnp.int32)
            pairs.append(stale[pl.ds(pl.multiple_of(place * PATCH, PATCH), PATCH), lanes])
        pairs.append(stale[PATCHES * PATCH :, lanes])
        scores = [nt_dot(query, part) for part in pairs]
        top = functools.reduce(
            jnp.maximum, [jnp.max(part, axis=-1, keepdims=True) for part in scores]
        )
        exponent = [jnp.exp(part - top) for part in scores]
        norm = sum(jnp.sum(part, axis=-1, keepdims=True) for part in exponent)
        values = sum(
            jnp.dot(part.astype(jnp.bfloat16), kv, preferred_element_type=jnp.float32)
            for part, kv in zip(exponent, pairs)
        )
        mixed.append((values[:, HD:] / norm).astype(jnp.bfloat16))
    terms = nt_dot(jnp.concatenate(mixed, axis=1), w_out[...])

    @pl.when(step == 0)
    def _():
        total[...] = terms

    @pl.when(step > 0)
    def _():
        total[...] += terms

    @pl.when(step == pl.num_programs(0) - 1)
    def _():
        out_terms[...] = total[...].astype(jnp.bfloat16)


def run_layer(facts, hidden, modulation, w_qkv, stale_kv, w_out, fresh_buf):
    width = hidden.shape[1]
    heads_here = stale_kv.shape[-1] // (2 * HD)
    block_heads = 4 if heads_here % 4 == 0 else heads_here
    items = modulation.shape[0]
    operands = [facts, hidden, modulation, w_qkv, stale_kv, w_out]
    in_specs = [
        pl.BlockSpec((PATCH, width), lambda i, f: (0, 0)),
        pl.BlockSpec((None, 3, width), lambda i, f: (f[0], 0, 0)),
        pl.BlockSpec((width, block_heads * 3 * HD), lambda i, f: (0, i)),
        pl.BlockSpec(
            (None, None, None, STALE, block_heads * 2 * HD),
            lambda i, f: (0, f[0] // 2, f[0] % 2, 0, i),
        ),
        pl.BlockSpec((width, block_heads * HD), lambda i, f: (0, i)),
    ]
    aliases = {}
    if fresh_buf is not None:
        aliases = {len(operands): 0}
        operands.append(fresh_buf)
        in_specs.append(pl.BlockSpec(memory_space=pl.ANY))
    return pl.pallas_call(
        functools.partial(layer_kernel, block_heads),
        out_shape=(
            jax.ShapeDtypeStruct((items, PATCH, heads_here * 2 * HD), jnp.bfloat16),
            jax.ShapeDtypeStruct((PATCH, width), jnp.bfloat16),
        ),
        grid_spec=pltpu.PrefetchScalarGridSpec(
            num_scalar_prefetch=1,
            grid=(heads_here // block_heads,),
            in_specs=in_specs,
            out_specs=[
                pl.BlockSpec((None, PATCH, block_heads * 2 * HD), lambda i, f: (f[0], 0, i)),
                pl.BlockSpec((PATCH, width), lambda i, f: (0, 0)),
            ],
            scratch_shapes=[
                pltpu.VMEM((PATCH, width), jnp.bfloat16),
                pltpu.VMEM((PATCH, width), jnp.float32),
            ],
        ),
        input_output_aliases=aliases,
        compiler_params=pltpu.CompilerParams(vmem_limit_bytes=48 << 20),
    )(*operands)


def shards(
    latent_tokens, w_qkv, w_out, time_mod, text_mod, stale_kv, guided, patch_index, timestep
):
    section_index = lax.axis_index("section")
    sections = lax.axis_size("section")
    requests = latent_tokens.shape[0]
    item_count = 2 * requests
    local_rows, model_width = latent_tokens.shape[2:]
    tokens = latent_tokens.reshape(item_count, local_rows, model_width)
    tokens_full = lax.all_gather(tokens, "head", axis=1, tiled=True)
    per_time = jnp.stack(
        [
            lax.dynamic_index_in_dim(time_mod[0], timestep[i], 0, keepdims=False)
            for i in range(requests)
        ]
    )
    modulation = (per_time[:, None] + text_mod[0]).reshape(item_count, 3, model_width)
    patch_all = jnp.repeat(patch_index, 2)
    guided_all = jnp.repeat(guided, 2)
    parity = jnp.arange(item_count, dtype=jnp.int32) % 2
    keep_all = jnp.where((parity == 1) & (guided_all == 0), 0, 1).astype(jnp.int32)
    qkv_all, out_all = gather_weights(w_qkv[0], w_out[0].T)
    qkv_full = qkv_all.reshape(-1, qkv_all.shape[-1])
    out_full = out_all.reshape(-1, out_all.shape[-1])

    fresh_buf = None
    received = None
    kept = []
    for tick in range(item_count + sections - 1):
        slot = jnp.clip(tick - section_index, 0, item_count - 1)
        layer_in = lax.dynamic_index_in_dim(tokens, slot, 0, keepdims=False)
        hidden = lax.dynamic_index_in_dim(tokens_full, slot, 0, keepdims=False)
        if tick > 0:
            arrived = lax.all_gather(received, "head", axis=0, tiled=True)
            layer_in = jnp.where(section_index == 0, layer_in, received)
            hidden = jnp.where(section_index == 0, hidden, arrived)
        facts = jnp.stack([slot, patch_all[slot], keep_all[slot]]).astype(jnp.int32)
        fresh_buf, out_terms = run_layer(
            facts, hidden, modulation, qkv_full, stale_kv, out_full, fresh_buf
        )
        attn = lax.psum_scatter(out_terms, "head", scatter_dimension=0, tiled=True)
        gate = lax.dynamic_index_in_dim(modulation[:, 2], slot, 0, keepdims=True)
        updated = (
            layer_in.astype(jnp.float32) + gate * attn.astype(jnp.float32)
        ).astype(jnp.bfloat16)
        kept.append(jnp.where(keep_all[slot] == 1, updated, jnp.zeros_like(updated)))
        if tick < item_count + sections - 2:
            received = lax.ppermute(
                updated, "section", [(i, i + 1) for i in range(sections - 1)]
            )
    hidden_out = jnp.stack(
        [jnp.where(section_index == 0, kept[i], kept[i + 1]) for i in range(item_count)]
    ).reshape(1, requests, 2, local_rows, model_width)
    fresh_kv = fresh_buf.reshape(1, requests, 2, PATCH, fresh_buf.shape[-1])
    return (hidden_out, fresh_kv)


def solution(mesh):
    in_specs = (
        P("req", None, "head", None),
        P("section", "req", "head"),
        P("section", "head", "req"),
        P("section", None, None, None),
        P("section", "req", None, None, None),
        P("section", "req", None, None, "head"),
        P("req"),
        P("req"),
        P("req"),
    )
    out_specs = (P("section", "req", None, "head", None), P("section", "req", None, None, "head"))
    return jax.shard_map(shards, mesh=mesh, in_specs=in_specs, out_specs=out_specs, check_vma=False)
```

time: 412 us -> 237 us (0.58)
  Pallas kernels: 0 us -> 140 us
  waiting for transfers between devices: 158 us -> 43.4 us
  other arithmetic: 86.1 us -> 9.36 us
  matrix products: 72.6 us -> 0 us
  local copies, waits for them, and re-layouts: 59.1 us -> 12.5 us
    pallas_call x0 -> x4, Pallas kernels: none -> 140 us  [the longest x1 94.2 us: gather_weights(): pl.pallas_call(functools.partial(gather_kernel, n), out_shape=(jax.ShapeD...]
    all_gather x2 -> x1, waiting for transfers between devices: 139 us -> 0.02 us  [shards(): tokens_full = lax.all_gather(tokens, 'head', axis=1, tiled=True)]
    dot_general x13 -> x0, matrix products: 72.6 us -> none  [the longest x3 25.5 us: attend(): jnp.einsum('qhd,khd->hqk', queries, all_keys, preferred_element_type=jnp....]
    sub x3 -> x0, other arithmetic: 63.7 us -> none  [attend(): exponent = jnp.exp(scores - row_max)]
    dynamic_slice x18 -> x3, local copies, waits for them, and re-layouts: 20.3 us -> 0.74 us  [the longest x1 0.68 us: shards(): keep_all[slot] == 1]
    reduce_scatter x3, waiting for transfers between devices: 12.8 us -> 27.1 us  [shards(): attn = lax.psum_scatter(out_terms, 'head', scatter_dimension=0, tiled=True)]
    unnamed x6 -> x22, local copies, waits for them, and re-layouts: 24.3 us -> 10.6 us
    ppermute x3 -> x2, waiting for transfers between devices: 5.16 us -> 15.5 us  [shards(): lax.ppermute(updated, 'section', [(i, i + 1) for i in range(sections - 1)])]
  transfers between devices with their start and end apart: 8 -> 6, of which waited for: 8 -> 5; matrix products, arithmetic and copies ran while one was open for 15% -> 4% of each run, Pallas kernels for 0% -> 40%
where the time goes in v1:
time: 237 us; the launch traced here: 236 us
  Pallas kernels  140 us (59%)
  waiting for transfers between devices  43.4 us (18%)
  between operations  17.8 us (8%)
  local copies, waits for them, and re-layouts  12.5 us (5%)
  other arithmetic  9.36 us (4%)
  starting transfers between devices  8.26 us (3%)
  blocking collectives  5.1 us (2%)
    pallas_call x1, Pallas kernels, gather_weights(): pl.pallas_call(functools.partial(gather_kernel, n), out_shape=(jax.ShapeD...  94.2 us
    pallas_call x3, Pallas kernels, run_layer(): pl.pallas_call(functools.partial(layer_kernel, block_heads), out_shape=(j...  45.7 us
    reduce_scatter x3, waiting for transfers between devices, shards(): attn = lax.psum_scatter(out_terms, 'head', scatter_dimension=0, tiled=True)  27.1 us
    ppermute x2, waiting for transfers between devices, shards(): lax.ppermute(updated, 'section', [(i, i + 1) for i in range(sections - 1)])  15.5 us
    unnamed x22, local copies, waits for them, and re-layouts  10.6 us
    ppermute x2, starting transfers between devices, shards(): lax.ppermute(updated, 'section', [(i, i + 1) for i in range(sections - 1)])  8.1 us
    all_gather x2, blocking collectives, shards(): arrived = lax.all_gather(received, 'head', axis=0, tiled=True)  5.1 us
  transfers between devices with their start and end apart: 6, of which 5 were waited for; matrix products, arithmetic and copies ran while one was open for 4% of the time, Pallas kernels for 40%

profile of v1, /device:TPU:0, one launch (start us, length us, event | category | flops | bytes accessed | tf_op | source)
XLA Modules:
  0.0 236.4 jit_solution(4051086205245933848)
XLA Ops:
  10.0 7.1 %copy.14.stale = bf16[1,1,2,1178,1536]{4,3,2,1,0:T(8,128)(2,1)} copy(bf16[1,1,2,1178,1536]{4,2,3,1,0:T(2,128)(2,1)} %param.14) | data formatting | bytes 14475264 | tf_op args[5]
  17.1 94.2 %shard_map.104 = (bf16[8,192,2304]{2,1,0:T(8,128)(2,1)}, bf16[8,192,768]{2,1,0:T(8,128)(2,1)}) custom-call(bf16[192,2304]{1,0:T(8,128)(2,1)} %bitcast.54, bf16[192,768]{1,0:T(8,128)(2,1)} %bitcast.55), custom_call_target="tpu_custom_call" | custom-call | tf_op jit(solution)/shard_map/pallas_call | solution.py:86
  112.0 0.8 pad_add_fusion.facts
  112.8 1.2 dynamic-slice_bitcast_fusion.hidden
  114.1 1.7 copy-done.1
  115.7 15.4 %shard_map.105 = (bf16[2,256,1536]{2,1,0:T(8,128)(2,1)}, bf16[256,1536]{1,0:T(8,128)(2,1)}) custom-call(s32[3]{0:T(128)S(1)} %pad_add_fusion.facts, bf16[256,1536]{1,0:T(8,128)(2,1)S(1)} %dynamic-slice_bitcast_fusion.hidden, f32[2,3,1536]{2,1,0:T(4,128)S(1)} %bitcast_add_fusion.mod, bf16[1536,2304]{1,0:T(8,128)(2,1)} %bitcast.50, ...), custom_call_target="tpu_custom_call" | custom-call | tf_op jit(solution)/shard_map/pallas_call | solution.py:187
  131.3 8.4 %reduce-scatter.4.cloned.1.call-done = bf16[128,1536]{1,0:T(8,128)(2,1)} async-done(((bf16[256,1536]{1,0:T(8,128)(2,1)}), bf16[128,1536]{1,0:T(8,128)(2,1)}) %reduce-scatter.4.cloned.1.call-update) | async-done | bytes 393232 | tf_op jit(solution)/shard_map/reduce_scatter | solution.py:251
  139.6 1.1 fusion
  140.8 4.4 %collective-permute-start = (bf16[128,1536]{1,0:T(8,128)(2,1)S(1)}, bf16[128,1536]{1,0:T(8,128)(2,1)}, u32[]{:S(2)}, u32[]{:S(2)}) collective-permute-start(bf16[128,1536]{1,0:T(8,128)(2,1)S(1)} %fusion), channel_id=1, source_target_pairs={{0,16},{1,17},{2,18},{3,19},{4,20},{5,21},{6,22},{7,23},{8,24},{9,... | collective-permute-start | bytes 1179656 | tf_op jit(solution)/shard_map/ppermute | solution.py:258
  145.9 7.4 %collective-permute-done = bf16[128,1536]{1,0:T(8,128)(2,1)} collective-permute-done((bf16[128,1536]{1,0:T(8,128)(2,1)S(1)}, bf16[128,1536]{1,0:T(8,128)(2,1)}, u32[]{:S(2)}, u32[]{:S(2)}) %collective-permute-start) | collective-permute-done | bytes 393248 | tf_op jit(solution)/shard_map/ppermute | solution.py:258
  153.2 2.6 %all_gather.10 = bf16[256,1536]{1,0:T(8,128)(2,1)S(1)} all-gather(bf16[128,1536]{1,0:T(8,128)(2,1)} %collective-permute-done), channel_id=1, replica_groups=mesh['section'=2,'req'=8,'head'=2] {'head'}, dimensions={0}, use_global_device_ids=true | all-gather | bytes 1179648 | tf_op jit(solution)/shard_map/all_gather | solution.py:244
  155.8 1.3 bitcast_select_fusion.1.hidden
  157.1 15.1 %shard_map.106 = (bf16[2,256,1536]{2,1,0:T(8,128)(2,1)}, bf16[256,1536]{1,0:T(8,128)(2,1)S(1)}) custom-call(s32[3]{0:T(128)S(1)} %pad_add_fusion.1.facts, bf16[256,1536]{1,0:T(8,128)(2,1)S(1)} %bitcast_select_fusion.1.hidden, f32[2,3,1536]{2,1,0:T(4,128)S(1)} %bitcast_add_fusion.mod, bf16[1536,2304]{1,0:T(8,128)(2,1)} %bitcast.51, ...), custom_call_target="tpu_custom_call", output_to_operand_aliasing={{0}: (6, {})} | custom-call | tf_op jit(solution)/shard_map/pallas_call | solution.py:187
  172.2 0.9 copy-done.4
  174.5 9.1 %reduce-scatter.6.cloned.1.call-done = bf16[128,1536]{1,0:T(8,128)(2,1)} async-done(((bf16[256,1536]{1,0:T(8,128)(2,1)}), bf16[128,1536]{1,0:T(8,128)(2,1)}) %reduce-scatter.6.cloned.1.call-update) | async-done | bytes 393232 | tf_op jit(solution)/shard_map/reduce_scatter | solution.py:251
  183.6 2.3 select_bitcast_fusion
  185.9 3.7 %collective-permute-start.1 = (bf16[128,1536]{1,0:T(8,128)(2,1)S(1)}, bf16[128,1536]{1,0:T(8,128)(2,1)S(1)}, u32[]{:S(2)}, u32[]{:S(2)}) collective-permute-start(bf16[128,1536]{1,0:T(8,128)(2,1)S(1)} %get-tuple-element.22), channel_id=1, source_target_pairs={{0,16},{1,17},{2,18},{3,19},{4,20},{5,21},{6,22},{7,23},{8,24},{9,... | collective-permute-start | bytes 1179656 | tf_op jit(solution)/shard_map/ppermute | solution.py:258
  190.3 8.1 %collective-permute-done.1 = bf16[128,1536]{1,0:T(8,128)(2,1)S(1)} collective-permute-done((bf16[128,1536]{1,0:T(8,128)(2,1)S(1)}, bf16[128,1536]{1,0:T(8,128)(2,1)S(1)}, u32[]{:S(2)}, u32[]{:S(2)}) %collective-permute-start.1) | collective-permute-done | bytes 393248 | tf_op jit(solution)/shard_map/ppermute | solution.py:258
  198.4 2.5 %all_gather.11 = bf16[256,1536]{1,0:T(8,128)(2,1)S(1)} all-gather(bf16[128,1536]{1,0:T(8,128)(2,1)S(1)} %collective-permute-done.1), channel_id=1, replica_groups=mesh['section'=2,'req'=8,'head'=2] {'head'}, dimensions={0}, use_global_device_ids=true | all-gather | bytes 1179648 | tf_op jit(solution)/shard_map/all_gather | solution.py:244
  201.1 15.1 %shard_map.107 = (bf16[2,256,1536]{2,1,0:T(8,128)(2,1)}, bf16[256,1536]{1,0:T(8,128)(2,1)S(1)}) custom-call(s32[3]{0:T(128)S(1)} %pad_add_fusion.2.facts, bf16[256,1536]{1,0:T(8,128)(2,1)S(1)} %bitcast_select_fusion.hidden, f32[2,3,1536]{2,1,0:T(4,128)S(1)} %bitcast_add_fusion.mod, bf16[1536,2304]{1,0:T(8,128)(2,1)} %bitcast.52, ...), custom_call_target="tpu_custom_call", output_to_operand_aliasing={{0}: (6, {})} | custom-call | tf_op jit(solution)/shard_map/pallas_call | solution.py:187
  216.2 0.9 copy-done.3
  217.8 9.7 %reduce-scatter.8.cloned.1.call-done = bf16[128,1536]{1,0:T(8,128)(2,1)} async-done(((bf16[256,1536]{1,0:T(8,128)(2,1)}), bf16[128,1536]{1,0:T(8,128)(2,1)}) %reduce-scatter.8.cloned.1.call-update) | async-done | bytes 393232 | tf_op jit(solution)/shard_map/reduce_scatter | solution.py:251
  227.5 1.4 fusion.3
  228.9 0.9 maximum_bitcast_fusion
  (36 shorter events, 3.2 us)
Async XLA Ops:
  7.2 2.7 %copy-start = (f32[1,28,3,1536]{3,0,2,1:T(1,128)S(1)}, f32[1,28,3,1536]{3,0,2,1:T(1,128)}, u32[]{:S(2)}) copy-start(f32[1,28,3,1536]{3,0,2,1:T(1,128)} %param.12) | copy-start | bytes 1548292
  7.2 105.7 %all-gather.3.cloned.1.call-start = ((), (), s32[]{:S(2)}) async-start(), calls=%async_computation.6 | async-start | bytes 2359296 | tf_op jit(solution)/shard_map/all_gather | solution.py:220
  7.9 131.7 %reduce-scatter.4.cloned.1.call-start = ((), (), s32[]{:S(2)}) async-start(), calls=%async_computation.3 | async-start | bytes 1179648 | tf_op jit(solution)/shard_map/reduce_scatter | solution.py:251
  10.0 102.8 %copy-start.9 = (f32[1,1,2,3,1536]{4,2,3,1,0:T(2,128)S(1)}, f32[1,1,2,3,1536]{4,2,3,1,0:T(2,128)}, u32[]{:S(2)}) copy-start(f32[1,1,2,3,1536]{4,2,3,1,0:T(2,128)} %param.13) | copy-start | bytes 110596
  114.0 1.7 copy-start.1
  115.7 23.9 %copy-start.5 = (bf16[1,2,128,1536]{3,2,1,0:T(8,128)(2,1)S(1)}, bf16[1,2,128,1536]{3,2,1,0:T(8,128)(2,1)}, u32[]{:S(2)}) copy-start(bf16[1,2,128,1536]{3,2,1,0:T(8,128)(2,1)} %param.9) | copy-start | bytes 2359300
  131.1 52.4 %reduce-scatter.6.cloned.1.call-start = ((), (), s32[]{:S(2)}) async-start(), calls=%async_computation.4 | async-start | bytes 1179648 | tf_op jit(solution)/shard_map/reduce_scatter | solution.py:251
  140.8 12.5 %collective-permute-start = (bf16[128,1536]{1,0:T(8,128)(2,1)S(1)}, bf16[128,1536]{1,0:T(8,128)(2,1)}, u32[]{:S(2)}, u32[]{:S(2)}) collective-permute-start(bf16[128,1536]{1,0:T(8,128)(2,1)S(1)} %fusion), channel_id=1, source_target_pairs={{0,16},{1,17},{2,18},{3,19},{4,20},{5,21},{6,22},{7,23},{8,24},{9,... | collective-permute-start | bytes 1179656 | tf_op jit(solution)/shard_map/ppermute | solution.py:258
  145.9 11.2 %copy-start.2 = (bf16[8,192,768]{2,1,0:T(8,128)(2,1)S(1)}, bf16[8,192,768]{2,1,0:T(8,128)(2,1)}, u32[]{:S(2)}) copy-start(bf16[8,192,768]{2,1,0:T(8,128)(2,1)} %get-tuple-element.11) | copy-start | bytes 7077892
  172.2 0.9 copy-start.4
  173.1 54.3 %reduce-scatter.8.cloned.1.call-start = ((), (), s32[]{:S(2)}) async-start(), calls=%async_computation.5 | async-start | bytes 1179648 | tf_op jit(solution)/shard_map/reduce_scatter | solution.py:251
  183.6 17.4 %copy-start.6 = (bf16[1,2,256,1536]{3,2,1,0:T(8,128)(2,1)S(1)}, bf16[1,2,256,1536]{3,2,1,0:T(8,128)(2,1)}, u32[]{:S(2)}) copy-start(bf16[1,2,256,1536]{3,2,1,0:T(8,128)(2,1)} %all-gather.3.cloned.1.call-done) | copy-start | bytes 4718596
  185.9 12.6 %copy-start.8 = (bf16[128,1536]{1,0:T(8,128)(2,1)}, bf16[128,1536]{1,0:T(8,128)(2,1)S(1)}, u32[]{:S(2)}) copy-start(bf16[128,1536]{1,0:T(8,128)(2,1)S(1)} %get-tuple-element.22) | copy-start | bytes 1179652
  185.9 12.6 %collective-permute-start.1 = (bf16[128,1536]{1,0:T(8,128)(2,1)S(1)}, bf16[128,1536]{1,0:T(8,128)(2,1)S(1)}, u32[]{:S(2)}, u32[]{:S(2)}) collective-permute-start(bf16[128,1536]{1,0:T(8,128)(2,1)S(1)} %get-tuple-element.22), channel_id=1, source_target_pairs={{0,16},{1,17},{2,18},{3,19},{4,20},{5,21},{6,22},{7,23},{8,24},{9,... | collective-permute-start | bytes 1179656 | tf_op jit(solution)/shard_map/ppermute | solution.py:258
  216.2 0.9 copy-start.3
  217.1 11.8 %copy-start.7 = (bf16[1,128,1536]{2,1,0:T(8,128)(2,1)S(1)}, bf16[1,128,1536]{2,1,0:T(8,128)(2,1)}, u32[]{:S(2)}) copy-start(bf16[1,128,1536]{2,1,0:T(8,128)(2,1)} %get-tuple-element.21) | copy-start | bytes 1179652
Sparse Core Ops, SparseCore 0:
  9.6 12.4 all-gather.2
  131.3 8.3 reduce-scatter.3
  173.3 10.2 reduce-scatter.5
  217.2 10.1 reduce-scatter.7

commit v2 on v1

--- a/solution.py
+++ b/solution.py
@@ -105,7 +105,7 @@
 
 
 def layer_kernel(
-    block_heads, facts, hidden, mod, w_qkv, stale, w_out, *rest
+    block_heads, base, facts, hidden, mod, w_qkv, stale, w_out, *rest
 ):
     fresh_out, out_terms, normed, total = rest[-4:]
     step = pl.program_id(0)
@@ -122,8 +122,8 @@
     projected = jnp.dot(normed[...], w_qkv[...], preferred_element_type=jnp.float32).astype(
         jnp.bfloat16
     )
-    patch_here = facts[1]
-    keep = facts[2].astype(jnp.float32)
+    patch_here = facts[base + 1]
+    keep = facts[base + 2].astype(jnp.float32)
     blank = jnp.zeros((PATCH, HD), jnp.bfloat16)
     mixed = []
     for head in range(block_heads):
@@ -163,19 +163,20 @@
         out_terms[...] = total[...].astype(jnp.bfloat16)
 
 
-def run_layer(facts, hidden, modulation, w_qkv, stale_kv, w_out, fresh_buf):
-    width = hidden.shape[1]
+def run_layer(tick, facts, hidden, modulation, w_qkv, stale_kv, w_out, fresh_buf):
+    width = hidden.shape[2]
     heads_here = stale_kv.shape[-1] // (2 * HD)
     block_heads = 4 if heads_here % 4 == 0 else heads_here
     items = modulation.shape[0]
+    base = 3 * tick
     operands = [facts, hidden, modulation, w_qkv, stale_kv, w_out]
     in_specs = [
-        pl.BlockSpec((PATCH, width), lambda i, f: (0, 0)),
-        pl.BlockSpec((None, 3, width), lambda i, f: (f[0], 0, 0)),
+        pl.BlockSpec((None, PATCH, width), lambda i, f: (0, 0, 0)),
+        pl.BlockSpec((None, 3, width), lambda i, f: (f[base], 0, 0)),
         pl.BlockSpec((width, block_heads * 3 * HD), lambda i, f: (0, i)),
         pl.BlockSpec(
             (None, None, None, STALE, block_heads * 2 * HD),
-            lambda i, f: (0, f[0] // 2, f[0] % 2, 0, i),
+            lambda i, f: (0, f[base] // 2, f[base] % 2, 0, i),
         ),
         pl.BlockSpec((width, block_heads * HD), lambda i, f: (0, i)),
     ]
@@ -185,7 +186,7 @@
         operands.append(fresh_buf)
         in_specs.append(pl.BlockSpec(memory_space=pl.ANY))
     return pl.pallas_call(
-        functools.partial(layer_kernel, block_heads),
+        functools.partial(layer_kernel, block_heads, base),
         out_shape=(
             jax.ShapeDtypeStruct((items, PATCH, heads_here * 2 * HD), jnp.bfloat16),
             jax.ShapeDtypeStruct((PATCH, width), jnp.bfloat16),
@@ -195,7 +196,7 @@
             grid=(heads_here // block_heads,),
             in_specs=in_specs,
             out_specs=[
-                pl.BlockSpec((None, PATCH, block_heads * 2 * HD), lambda i, f: (f[0], 0, i)),
+                pl.BlockSpec((None, PATCH, block_heads * 2 * HD), lambda i, f: (f[base], 0, i)),
                 pl.BlockSpec((PATCH, width), lambda i, f: (0, 0)),
             ],
             scratch_shapes=[
@@ -206,6 +207,176 @@
         input_output_aliases=aliases,
         compiler_params=pltpu.CompilerParams(vmem_limit_bytes=48 << 20),
     )(*operands)
+
+
+def exchange_kernel(heads, sections, next_item, terms, hidden, mods, tokens, *rest):
+    sends = next_item is not None
+    if sends:
+        kept, following, mine, inbox, h_send, h_recv, s_send, s_recv, f_send, f_recv, o_sem = rest
+    else:
+        kept, inbox, h_send, h_recv = rest
+    me = lax.axis_index("head")
+    section = lax.axis_index("section")
+    rows = kept.shape[0]
+    chunks = max(1, rows // 32)
+    size = rows // chunks
+
+    barrier = pltpu.get_barrier_semaphore()
+    for far in range(1, heads):
+        peer = {"head": (me + far) % heads}
+        pl.semaphore_signal(barrier, inc=1, device_id=peer, device_id_type=MESH)
+    if sends:
+
+        @pl.when(section > 0)
+        def _():
+            peer = {"section": section - 1}
+            pl.semaphore_signal(barrier, inc=1, device_id=peer, device_id_type=MESH)
+
+    greeted = heads - 1
+    if sends:
+        greeted = greeted + (section < sections - 1).astype(jnp.int32)
+    pl.semaphore_wait(barrier, greeted)
+
+    def rows_of(device, chunk):
+        return pl.ds(pl.multiple_of(device * rows + chunk * size, size), size)
+
+    def share(far, chunk):
+        peer = (me + far) % heads
+        return pltpu.make_async_remote_copy(
+            src_ref=terms.at[rows_of(peer, chunk)],
+            dst_ref=inbox.at[far - 1, pl.ds(chunk * size, size)],
+            send_sem=h_send.at[far - 1, chunk],
+            recv_sem=h_recv.at[far - 1, chunk],
+            device_id={"head": peer},
+            device_id_type=MESH,
+        )
+
+    def onward(chunk):
+        return pltpu.make_async_remote_copy(
+            src_ref=mine.at[pl.ds(chunk * size, size)],
+            dst_ref=following.at[rows_of(me, chunk)],
+            send_sem=s_send.at[chunk],
+            recv_sem=s_recv.at[chunk],
+            device_id={"section": section + 1},
+            device_id_type=MESH,
+        )
+
+    def arrived(chunk):
+        return pltpu.make_async_remote_copy(
+            src_ref=mine.at[pl.ds(chunk * size, size)],
+            dst_ref=following.at[rows_of(me, chunk)],
+            send_sem=s_send.at[chunk],
+            recv_sem=s_recv.at[chunk],
+            device_id={"section": section - 1},
+            device_id_type=MESH,
+        )
+
+    def forward(far, chunk, owner):
+        return pltpu.make_async_remote_copy(
+            src_ref=following.at[rows_of(owner, chunk)],
+            dst_ref=following.at[rows_of(owner, chunk)],
+            send_sem=f_send.at[far - 1, chunk],
+            recv_sem=f_recv.at[far - 1, chunk],
+            device_id={"head": (me + far) % heads},
+            device_id_type=MESH,
+        )
+
+    for chunk in range(chunks):
+        for far in range(1, heads):
+            share(far, chunk).start()
+    if sends:
+        own = pltpu.make_async_copy(tokens.at[next_item], following, o_sem)
+
+        @pl.when(section == 0)
+        def _():
+            own.start()
+
+    gate = mods[0:1, :]
+    keep = mods[1:2, :]
+    for chunk in range(chunks):
+        attn = terms[rows_of(me, chunk), :].astype(jnp.float32)
+        for far in range(1, heads):
+            share(far, chunk).wait_recv()
+            attn = attn + inbox[far - 1, chunk * size : (chunk + 1) * size, :].astype(jnp.float32)
+        before = hidden[rows_of(me, chunk), :].astype(jnp.float32)
+        updated = (before + gate * attn).astype(jnp.bfloat16)
+        kept[chunk * size : (chunk + 1) * size, :] = (updated.astype(jnp.float32) * keep).astype(
+            jnp.bfloat16
+        )
+        if sends:
+            mine[chunk * size : (chunk + 1) * size, :] = updated
+
+            @pl.when(section < sections - 1)
+            def _():
+                onward(chunk).start()
+
+    if sends:
+
+        @pl.when(section > 0)
+        def _():
+            for chunk in range(chunks):
+                arrived(chunk).wait_recv()
+                for far in range(1, heads):
+                    forward(far, chunk, me).start()
+            for chunk in range(chunks):
+                for far in range(1, heads):
+                    forward(far, chunk, (me + heads - far) % heads).wait_recv()
+                    forward(far, chunk, me).wait_send()
+
+        @pl.when(section < sections - 1)
+        def _():
+            for chunk in range(chunks):
+                onward(chunk).wait_send()
+
+        @pl.when(section == 0)
+        def _():
+            own.wait()
+
+    for chunk in range(chunks):
+        for far in range(1, heads):
+            share(far, chunk).wait_send()
+
+
+def exchange(tick, next_item, terms, hidden, mods, tokens):
+    heads = lax.axis_size("head")
+    sections = lax.axis_size("section")
+    width = terms.shape[1]
+    rows = PATCH // heads
+    chunks = max(1, rows // 32)
+    vmem = pl.BlockSpec(memory_space=pltpu.VMEM)
+    dma = pltpu.SemaphoreType.DMA
+    out_shape = [jax.ShapeDtypeStruct((rows, width), jnp.bfloat16)]
+    scratch = [
+        pltpu.VMEM((heads - 1, rows, width), jnp.bfloat16),
+        dma((heads - 1, chunks)),
+        dma((heads - 1, chunks)),
+    ]
+    if next_item is not None:
+        out_shape.append(jax.ShapeDtypeStruct((PATCH, width), jnp.bfloat16))
+        scratch = [
+            pltpu.VMEM((rows, width), jnp.bfloat16),
+            *scratch,
+            dma((chunks,)),
+            dma((chunks,)),
+            dma((heads - 1, chunks)),
+            dma((heads - 1, chunks)),
+            dma,
+        ]
+    return pl.pallas_call(
+        functools.partial(exchange_kernel, heads, sections, next_item),
+        out_shape=out_shape,
+        in_specs=[
+            vmem,
+            vmem,
+            vmem,
+            pl.BlockSpec(memory_space=pl.ANY),
+        ],
+        out_specs=[vmem] * len(out_shape),
+        scratch_shapes=scratch,
+        compiler_params=pltpu.CompilerParams(
+            collective_id=1 + tick, has_side_effects=True, vmem_limit_bytes=32 << 20
+        ),
+    )(terms, hidden, mods, tokens)
 
 
 def shards(
@@ -233,33 +404,37 @@
     qkv_full = qkv_all.reshape(-1, qkv_all.shape[-1])
     out_full = out_all.reshape(-1, out_all.shape[-1])
 
+    ticks = item_count + sections - 1
+    slots = [jnp.clip(tick - section_index, 0, item_count - 1) for tick in range(ticks)]
+    facts = jnp.stack([part for s in slots for part in (s, patch_all[s], keep_all[s])])
+    mods = [
+        jnp.stack(
+            [
+                lax.dynamic_index_in_dim(modulation[:, 2], s, 0, keepdims=False),
+                jnp.full((model_width,), keep_all[s].astype(jnp.float32)),
+            ]
+        )
+        for s in slots
+    ]
     fresh_buf = None
-    received = None
+    hidden = tokens_full
     kept = []
-    for tick in range(item_count + sections - 1):
-        slot = jnp.clip(tick - section_index, 0, item_count - 1)
-        layer_in = lax.dynamic_index_in_dim(tokens, slot, 0, keepdims=False)
-        hidden = lax.dynamic_index_in_dim(tokens_full, slot, 0, keepdims=False)
-        if tick > 0:
-            arrived = lax.all_gather(received, "head", axis=0, tiled=True)
-            layer_in = jnp.where(section_index == 0, layer_in, received)
-            hidden = jnp.where(section_index == 0, hidden, arrived)
-        facts = jnp.stack([slot, patch_all[slot], keep_all[slot]]).astype(jnp.int32)
+    for tick in range(ticks):
         fresh_buf, out_terms = run_layer(
-            facts, hidden, modulation, qkv_full, stale_kv, out_full, fresh_buf
-        )
-        attn = lax.psum_scatter(out_terms, "head", scatter_dimension=0, tiled=True)
-        gate = lax.dynamic_index_in_dim(modulation[:, 2], slot, 0, keepdims=True)
-        updated = (
-            layer_in.astype(jnp.float32) + gate * attn.astype(jnp.float32)
-        ).astype(jnp.bfloat16)
-        kept.append(jnp.where(keep_all[slot] == 1, updated, jnp.zeros_like(updated)))
-        if tick < item_count + sections - 2:
-            received = lax.ppermute(
-                updated, "section", [(i, i + 1) for i in range(sections - 1)]
-            )
+            tick, facts, hidden, modulation, qkv_full, stale_kv, out_full, fresh_buf
+        )
+        next_item = min(tick + 1, item_count - 1) if tick < ticks - 1 else None
+        result = exchange(tick, next_item, out_terms, hidden[0], mods[tick], tokens_full)
+        kept.append(result[0])
+        if next_item is not None:
+            hidden = result[1][None]
     hidden_out = jnp.stack(
-        [jnp.where(section_index == 0, kept[i], kept[i + 1]) for i in range(item_count)]
+        [
+            lax.select_n(section_index, *(kept[i + s] for s in range(sections)))
+            if sections > 2
+            else jnp.where(section_index == 0, kept[i], kept[i + sections - 1])
+            for i in range(item_count)
+        ]
     ).reshape(1, requests, 2, local_rows, model_width)
     fresh_kv = fresh_buf.reshape(1, requests, 2, PATCH, fresh_buf.shape[-1])
     return (hidden_out, fresh_kv)

time: 237 us -> 201 us (0.85)
  waiting for transfers between devices: 43.4 us -> 0.68 us
  Pallas kernels: 140 us -> 167 us
  other arithmetic: 9.36 us -> 1.04 us
  starting transfers between devices: 8.26 us -> 0.04 us
  blocking collectives: 5.1 us -> 0 us
    reduce_scatter x3 -> x0, waiting for transfers between devices: 27.1 us -> none  [shards(): attn = lax.psum_scatter(out_terms, 'head', scatter_dimension=0, tiled=True)]
    pallas_call x3 -> x6, Pallas kernels: 45.7 us -> 72.2 us  [the longest x3 45.4 us: run_layer(): pl.pallas_call(functools.partial(layer_kernel, block_heads, base), out_sh...]
    ppermute x2 -> x0, waiting for transfers between devices: 15.5 us -> none  [shards(): lax.ppermute(updated, 'section', [(i, i + 1) for i in range(sections - 1)])]
    ppermute x2 -> x0, starting transfers between devices: 8.1 us -> none  [shards(): lax.ppermute(updated, 'section', [(i, i + 1) for i in range(sections - 1)])]
    another operation x5 -> x1, other arithmetic: 5.87 us -> 0.07 us  [shards(): jnp.stack([lax.select_n(section_index, *(kept[i + s] for s in range(secti...]
    all_gather x2 -> x0, blocking collectives: 5.1 us -> none  [shards(): arrived = lax.all_gather(received, 'head', axis=0, tiled=True)]
    unnamed x22 -> x12, local copies, waits for them, and re-layouts: 10.6 us -> 10.2 us
  transfers between devices with their start and end apart: 6 -> 1, of which waited for: 5 -> 0; matrix products, arithmetic and copies ran while one was open for 4% -> 5% of each run, Pallas kernels for 40% -> 47%
where the time goes in v2:
time: 201 us; the launch traced here: 200 us
  Pallas kernels  167 us (83%)
  between operations  18.2 us (9%)
  local copies, waits for them, and re-layouts  13.1 us (7%)
    pallas_call x1, Pallas kernels, gather_weights(): pl.pallas_call(functools.partial(gather_kernel, n), out_shape=(jax.ShapeD...  94.3 us
    pallas_call x3, Pallas kernels, run_layer(): pl.pallas_call(functools.partial(layer_kernel, block_heads, base), out_sh...  45.4 us
    pallas_call x3, Pallas kernels, exchange(): pl.pallas_call(functools.partial(exchange_kernel, heads, sections, next_i...  26.8 us
    unnamed x12, local copies, waits for them, and re-layouts  10.2 us
  transfers between devices with their start and end apart: 1, of which 0 were waited for; matrix products, arithmetic and copies ran while one was open for 5% of the time, Pallas kernels for 47%

profile of v2, /device:TPU:0, one launch (start us, length us, event | category | flops | bytes accessed | tf_op | source)
XLA Modules:
  0.0 199.6 jit_solution(16055092514325262695)
XLA Ops:
  7.2 0.0 copy-start
  7.2 0.0 all-gather.3.cloned.1.call-start
  7.2 0.7 all-gather.3.cloned.1.call-update
  9.9 0.0 copy-done
  9.9 0.0 copy-start.4
  9.9 7.1 %copy.14.stale = bf16[1,1,2,1178,1536]{4,3,2,1,0:T(8,128)(2,1)} copy(bf16[1,1,2,1178,1536]{4,2,3,1,0:T(2,128)(2,1)} %param.14) | data formatting | bytes 14475264 | tf_op args[5]
  17.0 0.0 copy-done.4
  17.1 0.7 fusion
  19.8 94.3 %shard_map.104 = (bf16[8,192,2304]{2,1,0:T(8,128)(2,1)}, bf16[8,192,768]{2,1,0:T(8,128)(2,1)}) custom-call(bf16[192,2304]{1,0:T(8,128)(2,1)} %bitcast.53, bf16[192,768]{1,0:T(8,128)(2,1)} %bitcast.54), custom_call_target="tpu_custom_call" | custom-call | tf_op jit(solution)/shard_map/pallas_call | solution.py:86
  114.2 2.1 %stack.36.facts = s32[9]{0:T(128)S(1)} concatenate(s32[1]{0:T(128)} %bitcast, s32[1]{0:T(128)S(6)} %copy.24, s32[1]{0:T(128)} %get-tuple-element.33, s32[1]{0:T(128)} %bitcast.2, s32[1]{0:T(128)S(6)} %copy.24, s32[1]{0:T(128)} %get-tuple-element.32, s32[1]{0:T(128)} %bitcast.3, s32[1]{0:T(128)S(6)} %copy.24, s32[1]{0:T(128)} %get-tuple-element.31), dimensions={0} | concatenate | bytes 72 | tf_op jit(solution)/shard_map/stack | solution.py:409
  116.3 0.0 all-gather.3.cloned.1.call-done
  116.3 1.4 copy-done.1
  117.7 1.7 copy-done.3
  119.4 15.1 %shard_map.105 = (bf16[2,256,1536]{2,1,0:T(8,128)(2,1)}, bf16[256,1536]{1,0:T(8,128)(2,1)S(1)}) custom-call(s32[9]{0:T(128)S(1)} %stack.36.facts, bf16[2,256,1536]{2,1,0:T(8,128)(2,1)S(1)} %bitcast.40, f32[2,3,1536]{2,1,0:T(4,128)S(1)} %bitcast_add_fusion.mod, bf16[1536,2304]{1,0:T(8,128)(2,1)} %bitcast.49, bf16[1,1,2,1178,1536]{4,3,2,1,0:T(8,128)(2,1)} %copy.14.stale, ...), custom_call_target="tpu_custom_call" | custom-call | tf_op jit(solution)/shard_map/pallas_call | solution.py:188
  134.5 0.1 slice_bitcast_fusion.hidden
  134.6 10.9 %shard_map.106 = (bf16[128,1536]{1,0:T(8,128)(2,1)S(1)}, bf16[256,1536]{1,0:T(8,128)(2,1)S(1)}) custom-call(bf16[256,1536]{1,0:T(8,128)(2,1)S(1)} %get-tuple-element.16.terms, bf16[256,1536]{1,0:T(8,128)(2,1)S(1)} %slice_bitcast_fusion.hidden, f32[2,1536]{1,0:T(2,128)S(1)} %stack.37.mods, bf16[2,256,1536]{2,1,0:T(8,128)(2,1)S(1)} %bitcast.41), custom_call_target="tpu_custom_call" | custom-call | tf_op jit(solution)/shard_map/pallas_call | solution.py:365
  145.5 0.0 copy-start.2
  145.5 15.1 %shard_map.107 = (bf16[2,256,1536]{2,1,0:T(8,128)(2,1)}, bf16[256,1536]{1,0:T(8,128)(2,1)S(1)}) custom-call(s32[9]{0:T(128)S(1)} %stack.36.facts, bf16[1,256,1536]{2,1,0:T(8,128)(2,1)S(1)} %bitcast.48, f32[2,3,1536]{2,1,0:T(4,128)S(1)} %bitcast_add_fusion.mod, bf16[1536,2304]{1,0:T(8,128)(2,1)} %bitcast.50, ...), custom_call_target="tpu_custom_call", output_to_operand_aliasing={{0}: (6, {})} | custom-call | tf_op jit(solution)/shard_map/pallas_call | solution.py:188
  160.7 0.0 copy-done.2
  160.7 14.0 %shard_map.108 = (bf16[128,1536]{1,0:T(8,128)(2,1)S(1)}, bf16[256,1536]{1,0:T(8,128)(2,1)S(1)}) custom-call(bf16[256,1536]{1,0:T(8,128)(2,1)S(1)} %get-tuple-element.20.terms, bf16[256,1536]{1,0:T(8,128)(2,1)S(1)} %get-tuple-element.18.hidden, f32[2,1536]{1,0:T(2,128)S(1)} %stack.38.mods, bf16[2,256,1536]{2,1,0:T(8,128)(2,1)S(1)} %bitcast.42), custom_call_target="tpu_custom_call" | custom-call | tf_op jit(solution)/shard_map/pallas_call | solution.py:365
  174.7 15.1 %shard_map.109 = (bf16[2,256,1536]{2,1,0:T(8,128)(2,1)}, bf16[256,1536]{1,0:T(8,128)(2,1)S(1)}) custom-call(s32[9]{0:T(128)S(1)} %stack.36.facts, bf16[1,256,1536]{2,1,0:T(8,128)(2,1)S(1)} %bitcast.47, f32[2,3,1536]{2,1,0:T(4,128)S(1)} %bitcast_add_fusion.mod, bf16[1536,2304]{1,0:T(8,128)(2,1)} %bitcast.51, ...), custom_call_target="tpu_custom_call", output_to_operand_aliasing={{0}: (6, {})} | custom-call | tf_op jit(solution)/shard_map/pallas_call | solution.py:188
  189.8 1.9 shard_map.110
  191.7 0.1 select_bitcast_fusion.1
  191.8 0.9 maximum_bitcast_fusion
  (11 shorter events, 0.1 us)
Async XLA Ops:
  7.2 2.7 %copy-start = (f32[1,28,3,1536]{3,0,2,1:T(1,128)S(1)}, f32[1,28,3,1536]{3,0,2,1:T(1,128)}, u32[]{:S(2)}) copy-start(f32[1,28,3,1536]{3,0,2,1:T(1,128)} %param.12) | copy-start | bytes 1548292
  7.2 109.1 %all-gather.3.cloned.1.call-start = ((), (), s32[]{:S(2)}) async-start(), calls=%async_computation | async-start | bytes 2359296 | tf_op jit(solution)/shard_map/all_gather | solution.py:391
  9.9 7.1 %copy-start.4 = (f32[1,1,2,3,1536]{4,2,3,1,0:T(2,128)S(1)}, f32[1,1,2,3,1536]{4,2,3,1,0:T(2,128)}, u32[]{:S(2)}) copy-start(f32[1,1,2,3,1536]{4,2,3,1,0:T(2,128)} %param.13) | copy-start | bytes 110596
  116.3 1.4 copy-start.1
  117.7 1.7 copy-start.3
  145.5 15.2 %copy-start.2 = (bf16[1,2,256,1536]{3,2,1,0:T(8,128)(2,1)S(1)}, bf16[1,2,256,1536]{3,2,1,0:T(8,128)(2,1)}, u32[]{:S(2)}) copy-start(bf16[1,2,256,1536]{3,2,1,0:T(8,128)(2,1)} %all-gather.3.cloned.1.call-done) | copy-start | bytes 4718596
Sparse Core Ops, SparseCore 0:
  9.6 12.4 all-gather.2

commit v3 on v2

--- a/solution.py
+++ b/solution.py
@@ -166,7 +166,7 @@
 def run_layer(tick, facts, hidden, modulation, w_qkv, stale_kv, w_out, fresh_buf):
     width = hidden.shape[2]
     heads_here = stale_kv.shape[-1] // (2 * HD)
-    block_heads = 4 if heads_here % 4 == 0 else heads_here
+    block_heads = 6 if heads_here % 6 == 0 else heads_here
     items = modulation.shape[0]
     base = 3 * tick
     operands = [facts, hidden, modulation, w_qkv, stale_kv, w_out]
@@ -406,7 +406,16 @@
 
     ticks = item_count + sections - 1
     slots = [jnp.clip(tick - section_index, 0, item_count - 1) for tick in range(ticks)]
-    facts = jnp.stack([part for s in slots for part in (s, patch_all[s], keep_all[s])])
+    slot_all = jnp.clip(jnp.arange(ticks, dtype=jnp.int32) - section_index, 0, item_count - 1)
+    chosen = slot_all[:, None] == jnp.arange(item_count, dtype=jnp.int32)[None, :]
+    facts = jnp.stack(
+        [
+            slot_all,
+            jnp.sum(jnp.where(chosen, patch_all[None, :], 0), axis=1),
+            jnp.sum(jnp.where(chosen, keep_all[None, :], 0), axis=1),
+        ],
+        axis=1,
+    ).reshape(-1)
     mods = [
         jnp.stack(
             [

time: 201 us -> 199 us (0.990)
    another operation x1, local copies, waits for them, and re-layouts: 2.11 us -> 0.1 us  [shards(): jnp.stack([slot_all, jnp.sum(jnp.where(chosen, patch_all[None, :], 0), ax...]
  transfers between devices with their start and end apart: 1 -> 1, of which waited for: 0 -> 0; matrix products, arithmetic and copies ran while one was open for 5% -> 4% of each run, Pallas kernels for 47% -> 48%
where the time goes in v3:
time: 199 us; the launch traced here: 198 us
  Pallas kernels  167 us (84%)
  between operations  18 us (9%)
  local copies, waits for them, and re-layouts  11.1 us (6%)
    pallas_call x1, Pallas kernels, gather_weights(): pl.pallas_call(functools.partial(gather_kernel, n), out_shape=(jax.ShapeD...  94.3 us
    pallas_call x3, Pallas kernels, run_layer(): pl.pallas_call(functools.partial(layer_kernel, block_heads, base), out_sh...  45.2 us
    pallas_call x3, Pallas kernels, exchange(): pl.pallas_call(functools.partial(exchange_kernel, heads, sections, next_i...  27 us
    unnamed x12, local copies, waits for them, and re-layouts  10.2 us
  transfers between devices with their start and end apart: 1, of which 0 were waited for; matrix products, arithmetic and copies ran while one was open for 4% of the time, Pallas kernels for 48%

profile of v3, /device:TPU:0, one launch (start us, length us, event | category | flops | bytes accessed | tf_op | source)
XLA Modules:
  0.0 197.6 jit_solution(14042224036933335001)
XLA Ops:
  7.2 0.0 copy-start
  7.2 0.0 all-gather.3.cloned.1.call-start
  7.2 0.7 all-gather.3.cloned.1.call-update
  9.3 0.1 select_reduce_fusion.1
  9.4 0.1 copy.18
  9.4 0.1 reshape.69.facts
  10.2 0.0 copy-done
  10.2 0.0 copy-start.4
  10.2 7.1 %copy.20.stale = bf16[1,1,2,1178,1536]{4,3,2,1,0:T(8,128)(2,1)} copy(bf16[1,1,2,1178,1536]{4,2,3,1,0:T(2,128)(2,1)} %param.14) | data formatting | bytes 14475264 | tf_op args[5]
  17.4 0.0 copy-done.4
  17.4 0.6 fusion
  19.9 94.3 %shard_map.107 = (bf16[8,192,2304]{2,1,0:T(8,128)(2,1)}, bf16[8,192,768]{2,1,0:T(8,128)(2,1)}) custom-call(bf16[192,2304]{1,0:T(8,128)(2,1)} %bitcast.54, bf16[192,768]{1,0:T(8,128)(2,1)} %bitcast.55), custom_call_target="tpu_custom_call" | custom-call | tf_op jit(solution)/shard_map/pallas_call | solution.py:86
  114.3 0.0 all-gather.3.cloned.1.call-done
  114.3 1.4 copy-done.1
  115.7 1.7 copy-done.3
  117.4 15.1 %shard_map.108 = (bf16[2,256,1536]{2,1,0:T(8,128)(2,1)}, bf16[256,1536]{1,0:T(8,128)(2,1)S(1)}) custom-call(s32[9]{0:T(128)S(1)} %reshape.69.facts, bf16[2,256,1536]{2,1,0:T(8,128)(2,1)S(1)} %bitcast.41, f32[2,3,1536]{2,1,0:T(4,128)S(1)} %bitcast_add_fusion.mod, bf16[1536,2304]{1,0:T(8,128)(2,1)} %bitcast.50, bf16[1,1,2,1178,1536]{4,3,2,1,0:T(8,128)(2,1)} %copy.20.stale, ...), custom_call_target="tpu_custom_call" | custom-call | tf_op jit(solution)/shard_map/pallas_call | solution.py:188
  132.5 0.1 slice_bitcast_fusion.hidden
  132.5 11.3 %shard_map.109 = (bf16[128,1536]{1,0:T(8,128)(2,1)S(1)}, bf16[256,1536]{1,0:T(8,128)(2,1)S(1)}) custom-call(bf16[256,1536]{1,0:T(8,128)(2,1)S(1)} %get-tuple-element.16.terms, bf16[256,1536]{1,0:T(8,128)(2,1)S(1)} %slice_bitcast_fusion.hidden, f32[2,1536]{1,0:T(2,128)S(1)} %stack.34.mods, bf16[2,256,1536]{2,1,0:T(8,128)(2,1)S(1)} %bitcast.42), custom_call_target="tpu_custom_call" | custom-call | tf_op jit(solution)/shard_map/pallas_call | solution.py:365
  143.8 15.1 %shard_map.110 = (bf16[2,256,1536]{2,1,0:T(8,128)(2,1)}, bf16[256,1536]{1,0:T(8,128)(2,1)S(1)}) custom-call(s32[9]{0:T(128)S(1)} %reshape.69.facts, bf16[1,256,1536]{2,1,0:T(8,128)(2,1)S(1)} %bitcast.49, f32[2,3,1536]{2,1,0:T(4,128)S(1)} %bitcast_add_fusion.mod, bf16[1536,2304]{1,0:T(8,128)(2,1)} %bitcast.51, ...), custom_call_target="tpu_custom_call", output_to_operand_aliasing={{0}: (6, {})} | custom-call | tf_op jit(solution)/shard_map/pallas_call | solution.py:188
  158.9 13.9 %shard_map.111 = (bf16[128,1536]{1,0:T(8,128)(2,1)S(1)}, bf16[256,1536]{1,0:T(8,128)(2,1)S(1)}) custom-call(bf16[256,1536]{1,0:T(8,128)(2,1)S(1)} %get-tuple-element.20.terms, bf16[256,1536]{1,0:T(8,128)(2,1)S(1)} %get-tuple-element.18.hidden, f32[2,1536]{1,0:T(2,128)S(1)} %stack.35.mods, bf16[2,256,1536]{2,1,0:T(8,128)(2,1)S(1)} %bitcast.43), custom_call_target="tpu_custom_call" | custom-call | tf_op jit(solution)/shard_map/pallas_call | solution.py:365
  172.8 15.1 %shard_map.112 = (bf16[2,256,1536]{2,1,0:T(8,128)(2,1)}, bf16[256,1536]{1,0:T(8,128)(2,1)S(1)}) custom-call(s32[9]{0:T(128)S(1)} %reshape.69.facts, bf16[1,256,1536]{2,1,0:T(8,128)(2,1)S(1)} %bitcast.48, f32[2,3,1536]{2,1,0:T(4,128)S(1)} %bitcast_add_fusion.mod, bf16[1536,2304]{1,0:T(8,128)(2,1)} %bitcast.52, ...), custom_call_target="tpu_custom_call", output_to_operand_aliasing={{0}: (6, {})} | custom-call | tf_op jit(solution)/shard_map/pallas_call | solution.py:188
  187.8 1.9 shard_map.113
  189.7 0.1 select_bitcast_fusion.1
  189.8 0.9 maximum_bitcast_fusion
  (16 shorter events, 0.1 us)
Async XLA Ops:
  7.2 3.0 %copy-start = (f32[1,28,3,1536]{3,0,2,1:T(1,128)S(1)}, f32[1,28,3,1536]{3,0,2,1:T(1,128)}, u32[]{:S(2)}) copy-start(f32[1,28,3,1536]{3,0,2,1:T(1,128)} %param.12) | copy-start | bytes 1548292
  7.2 107.1 %all-gather.3.cloned.1.call-start = ((), (), s32[]{:S(2)}) async-start(), calls=%async_computation | async-start | bytes 2359296 | tf_op jit(solution)/shard_map/all_gather | solution.py:391
  10.2 7.1 %copy-start.4 = (f32[1,1,2,3,1536]{4,2,3,1,0:T(2,128)S(1)}, f32[1,1,2,3,1536]{4,2,3,1,0:T(2,128)}, u32[]{:S(2)}) copy-start(f32[1,1,2,3,1536]{4,2,3,1,0:T(2,128)} %param.13) | copy-start | bytes 110596
  114.3 1.4 copy-start.1
  115.7 1.7 copy-start.3
  143.8 15.1 %copy-start.2 = (bf16[1,2,256,1536]{3,2,1,0:T(8,128)(2,1)S(1)}, bf16[1,2,256,1536]{3,2,1,0:T(8,128)(2,1)}, u32[]{:S(2)}) copy-start(bf16[1,2,256,1536]{3,2,1,0:T(8,128)(2,1)} %all-gather.3.cloned.1.call-done) | copy-start | bytes 4718596
Sparse Core Ops, SparseCore 0:
  9.6 12.4 all-gather.2
